TPU v7x, 128 devices: a whole 4x4x4 slice. The times are simulated.
128 devices in a mesh: leaf: 8 (over x, core), prow: 4 (over z), pcol: 4 (over y).
Axes of the slice: x: 4, y: 4, z: 4, core: 2. Of those that a mesh axis runs over, the one named last changes fastest.
Arguments:
- subtree_factor: float32 [8, 2, 8, 256, 2048], P('leaf', None, None, 'prow', 'pcol'), may hold values from -0.09375 to 0.09375
- sub_linv: float32 [8, 2, 8, 256, 256], P('leaf', None, None, 'prow'), may hold values from -0.05 to 1.05
- sub_uinv: float32 [8, 2, 8, 256, 256], P('leaf', None, None, 'prow'), may hold values from -0.05 to 1.05
- lower_panel: float32 [8, 4, 256, 2, 2048], P('leaf', None, 'prow', None, 'pcol'), may hold values from -0.0234375 to 0.0234375
- upper_panel: float32 [8, 2, 8, 256, 1024], P('leaf', None, None, 'prow', 'pcol'), may hold values from -0.125 to 0.125
- panel_rows: int32 [8, 4, 2], P('leaf'), may hold values 0 or 1
- upper_level_factor: float32 [4, 256, 1024], P(None, 'prow', 'pcol'), may hold values from -0.125 to 0.125
- top_linv: float32 [4, 256, 256], P(None, 'prow'), may hold values from -0.05 to 1.05
- top_uinv: float32 [4, 256, 256], P(None, 'prow'), may hold values from -0.05 to 1.05
- sub_rhs: float32 [8, 2, 8, 256, 256], P('leaf', None, None, 'prow'), may hold values from -6 to 6
- top_rhs: float32 [4, 256, 256], P(None, 'prow', 'leaf'), may hold values from -6 to 6
Outputs:
- sub_solution: float32 [8, 2, 8, 256, 256], P('leaf', None, 'pcol')
- top_solution: float32 [4, 256, 256], P('pcol', None, 'leaf')
All inputs are finite; a program needn't handle non-finite values. No bound on the sum of `panel_rows` on one device may be relied on, other than what follows from the above.
Results may differ from a plain program's by a relative error of at most 0.00013.
Values sent between devices are 32-bit elements; how exact they have to be, the bound alone decides.
A program may use at most 128 MiB of HBM per device.

v0:
```python
import jax
import jax.numpy as jnp
from jax import lax
from jax.sharding import PartitionSpec as P

TOP_PRECISION = lax.Precision.HIGHEST


def block_order(block_count, forward):
    return range(block_count) if forward else range(block_count - 1, -1, -1)


def sweep_blocks(factor_row_block, inverses, right_side, coupling, owned_start, my_col, forward):
    groups, block_count, tile_rows, columns = right_side.shape
    block_rows = inverses.shape[3]
    owned_count = factor_row_block.shape[3] // block_rows
    solved = jnp.zeros((groups, block_count, block_rows, columns), jnp.float32)
    for sweep_step_index in block_order(block_count, forward):
        held_value_entries = lax.dynamic_slice_in_dim(solved, owned_start, owned_count, 1)
        held_value_entries = held_value_entries.reshape(groups, owned_count * block_rows, columns)
        partial_value = coupling[:, sweep_step_index] + jnp.einsum(
            "pht,ptj->phj",
            factor_row_block[:, sweep_step_index],
            held_value_entries,
            precision=TOP_PRECISION,
        )
        local_side = jnp.where(my_col == 0, right_side[:, sweep_step_index], 0.0) - partial_value
        inverse_part = jnp.einsum(
            "gab,gar->gbr", inverses[:, sweep_step_index], local_side, precision=TOP_PRECISION
        )
        block_value = lax.psum(inverse_part, ("prow", "pcol"))
        solved = solved.at[:, sweep_step_index].set(block_value)
    return solved


def per_device(
    subtree_factor,
    sub_linv,
    sub_uinv,
    lower_panel,
    upper_panel,
    panel_rows,
    upper_level_factor,
    top_linv,
    top_uinv,
    sub_rhs,
    top_rhs,
):
    my_row = lax.axis_index("prow")
    my_col = lax.axis_index("pcol")
    block_rows = sub_linv.shape[4]
    tile_rows = sub_rhs.shape[3]
    groups = sub_rhs.shape[1]
    block_count = sub_rhs.shape[2]
    sub_owned = subtree_factor.shape[4] // block_rows
    top_owned = upper_level_factor.shape[2] // block_rows
    present = panel_rows[0].astype(jnp.float32)
    linv_rows, uinv_rows, top_linv_rows, top_uinv_rows = (sub_linv, sub_uinv, top_linv, top_uinv)
    lower_sub = sweep_blocks(
        subtree_factor[0],
        linv_rows[0],
        sub_rhs[0],
        jnp.zeros(sub_rhs[0].shape, jnp.float32),
        my_col * sub_owned,
        my_col,
        True,
    )
    lower_owned = lax.dynamic_slice_in_dim(lower_sub, my_col * sub_owned, sub_owned, 1)
    lower_owned = lower_owned.reshape(groups, sub_owned * block_rows, lower_sub.shape[3])
    contrib_part = jnp.einsum(
        "tasm,ts,smr->tar", lower_panel[0], present, lower_owned, precision=TOP_PRECISION
    )
    contrib = lax.psum(contrib_part, "leaf")
    upper_level_side = lax.all_gather(top_rhs, "leaf", axis=2, tiled=True)
    upper_level_lower = sweep_blocks(
        upper_level_factor[None],
        top_linv_rows[None],
        upper_level_side[None],
        contrib[None],
        my_col * top_owned,
        my_col,
        True,
    )
    top_rows = lax.dynamic_slice_in_dim(upper_level_lower, my_row * tile_rows, tile_rows, 2)
    top_upper = sweep_blocks(
        upper_level_factor[None],
        top_uinv_rows[None],
        top_rows,
        jnp.zeros(top_rows.shape, jnp.float32),
        my_col * top_owned,
        my_col,
        False,
    )[0]
    top_out = lax.dynamic_slice_in_dim(
        top_upper, lax.axis_index("leaf") * top_rhs.shape[2], top_rhs.shape[2], 2
    )
    top_out = lax.dynamic_slice_in_dim(top_out, my_col * top_owned, top_owned, 0)
    top_mine = lax.dynamic_slice_in_dim(top_upper, my_col * top_owned, top_owned, 0)
    mask_mine = lax.dynamic_slice_in_dim(present, my_col * top_owned, top_owned, 0)
    upper_local = upper_panel[0].reshape(groups, block_count, tile_rows, top_owned, block_rows)
    coupling = jnp.einsum(
        "skatb,ts,tbr->skar", upper_local, mask_mine, top_mine, precision=TOP_PRECISION
    )
    sub_rows = lax.dynamic_slice_in_dim(lower_sub, my_row * tile_rows, tile_rows, 2)
    upper_sub = sweep_blocks(
        subtree_factor[0], uinv_rows[0], sub_rows, coupling, my_col * sub_owned, my_col, False
    )
    sub_out = lax.dynamic_slice_in_dim(upper_sub, my_col * sub_owned, sub_owned, 1)
    return (sub_out[None], top_out)


def solution(mesh):
    placed = (
        P("leaf", None, None, "prow", "pcol"),
        P("leaf", None, None, "prow", None),
        P("leaf", None, None, "prow", None),
        P("leaf", None, "prow", None, "pcol"),
        P("leaf", None, None, "prow", "pcol"),
        P("leaf", None, None),
        P(None, "prow", "pcol"),
        P(None, "prow", None),
        P(None, "prow", None),
        P("leaf", None, None, "prow", None),
        P(None, "prow", "leaf"),
    )
    return jax.shard_map(
        per_device,
        mesh=mesh,
        in_specs=placed,
        out_specs=(P("leaf", None, "pcol", None, None), P("pcol", None, "leaf")),
        check_vma=False,
    )
```

profile of v0, /device:TPU:0, one launch (start us, length us, event | category | flops | bytes accessed | tf_op | source)
XLA Modules:
  0.0 2303.5 jit_solution(17855429060302195027)
XLA Ops:
  15.9 88.4 %all-reduce.30.cloned.1.call-done = f32[2,1,256,256]{3,2,0,1:T(8,128)} async-done(((f32[2,1,256,256]{3,2,0,1:T(8,128)}), f32[2,1,256,256]{3,2,0,1:T(8,128)}) %all-reduce.30.cloned.1.call-update) | async-done | bytes 524304 | tf_op jit(solution)/shard_map/psum | solution.py:31
  109.6 3.4 scatter.80
  113.0 80.7 %all-reduce.32.cloned.1.call-done = f32[2,1,256,256]{3,2,0,1:T(8,128)} async-done(((f32[2,1,256,256]{3,2,0,1:T(8,128)}), f32[2,1,256,256]{3,2,0,1:T(8,128)}) %all-reduce.32.cloned.1.call-update) | async-done | bytes 524304 | tf_op jit(solution)/shard_map/psum | solution.py:31
  201.2 85.3 %all-reduce.34.cloned.1.call-done = f32[2,1,256,256]{3,2,0,1:T(8,128)} async-done(((f32[2,1,256,256]{3,2,0,1:T(8,128)}), f32[2,1,256,256]{3,2,0,1:T(8,128)}) %all-reduce.34.cloned.1.call-update) | async-done | bytes 524304 | tf_op jit(solution)/shard_map/psum | solution.py:31
  293.9 85.3 %all-reduce.36.cloned.1.call-done = f32[2,1,256,256]{3,2,0,1:T(8,128)} async-done(((f32[2,1,256,256]{3,2,0,1:T(8,128)}), f32[2,1,256,256]{3,2,0,1:T(8,128)}) %all-reduce.36.cloned.1.call-update) | async-done | bytes 524304 | tf_op jit(solution)/shard_map/psum | solution.py:31
  386.6 85.3 %all-reduce.38.cloned.1.call-done = f32[2,1,256,256]{3,2,0,1:T(8,128)} async-done(((f32[2,1,256,256]{3,2,0,1:T(8,128)}), f32[2,1,256,256]{3,2,0,1:T(8,128)}) %all-reduce.38.cloned.1.call-update) | async-done | bytes 524304 | tf_op jit(solution)/shard_map/psum | solution.py:31
  479.3 85.2 %all-reduce.40.cloned.1.call-done = f32[2,1,256,256]{3,2,0,1:T(8,128)} async-done(((f32[2,1,256,256]{3,2,0,1:T(8,128)}), f32[2,1,256,256]{3,2,0,1:T(8,128)}) %all-reduce.40.cloned.1.call-update) | async-done | bytes 524304 | tf_op jit(solution)/shard_map/psum | solution.py:31
  572.0 85.3 %all-reduce.42.cloned.1.call-done = f32[2,1,256,256]{3,2,0,1:T(8,128)} async-done(((f32[2,1,256,256]{3,2,0,1:T(8,128)}), f32[2,1,256,256]{3,2,0,1:T(8,128)}) %all-reduce.42.cloned.1.call-update) | async-done | bytes 524304 | tf_op jit(solution)/shard_map/psum | solution.py:31
  665.0 2.6 fusion.33
  667.6 82.2 %all-reduce.44.cloned.1.call-done = f32[2,1,256,256]{3,2,0,1:T(8,128)} async-done(((f32[2,1,256,256]{3,2,0,1:T(8,128)}), f32[2,1,256,256]{3,2,0,1:T(8,128)}) %all-reduce.44.cloned.1.call-update) | async-done | bytes 524304 | tf_op jit(solution)/shard_map/psum | solution.py:31
  755.1 14.6 all_gather.3
  771.9 42.9 %all-reduce.46.cloned.1.call-done = f32[1,4,64,256]{3,2,1,0:T(8,128)} async-done(((f32[1,4,64,256]{3,2,1,0:T(8,128)}), f32[1,4,64,256]{3,2,1,0:T(8,128)}) %all-reduce.46.cloned.1.call-update) | async-done | bytes 262160 | tf_op jit(solution)/shard_map/psum | solution.py:73
  816.8 85.7 %all-reduce.48.cloned.1.call-done = f32[1,1,256,256]{3,2,1,0:T(8,128)} async-done(((f32[1,1,256,256]{3,2,1,0:T(8,128)}), f32[1,1,256,256]{3,2,1,0:T(8,128)}) %all-reduce.48.cloned.1.call-update) | async-done | bytes 262160 | tf_op jit(solution)/shard_map/psum | solution.py:31
  907.9 82.4 %all-reduce.50.cloned.1.call-done = f32[1,1,256,256]{3,2,1,0:T(8,128)} async-done(((f32[1,1,256,256]{3,2,1,0:T(8,128)}), f32[1,1,256,256]{3,2,1,0:T(8,128)}) %all-reduce.50.cloned.1.call-update) | async-done | bytes 262160 | tf_op jit(solution)/shard_map/psum | solution.py:31
  995.2 84.5 %all-reduce.52.cloned.1.call-done = f32[1,1,256,256]{3,2,1,0:T(8,128)} async-done(((f32[1,1,256,256]{3,2,1,0:T(8,128)}), f32[1,1,256,256]{3,2,1,0:T(8,128)}) %all-reduce.52.cloned.1.call-update) | async-done | bytes 262160 | tf_op jit(solution)/shard_map/psum | solution.py:31
  1084.7 84.5 %all-reduce.54.cloned.1.call-done = f32[1,1,256,256]{3,2,1,0:T(8,128)} async-done(((f32[1,1,256,256]{3,2,1,0:T(8,128)}), f32[1,1,256,256]{3,2,1,0:T(8,128)}) %all-reduce.54.cloned.1.call-update) | async-done | bytes 262160 | tf_op jit(solution)/shard_map/psum | solution.py:31
  1173.0 84.5 %all-reduce.56.cloned.1.call-done = f32[1,1,256,256]{2,3,1,0:T(8,128)} async-done(((f32[1,1,256,256]{2,3,1,0:T(8,128)}), f32[1,1,256,256]{2,3,1,0:T(8,128)}) %all-reduce.56.cloned.1.call-update) | async-done | bytes 262160 | tf_op jit(solution)/shard_map/psum | solution.py:31
  1262.8 82.5 %all-reduce.58.cloned.1.call-done = f32[1,1,256,256]{2,3,1,0:T(8,128)} async-done(((f32[1,1,256,256]{2,3,1,0:T(8,128)}), f32[1,1,256,256]{2,3,1,0:T(8,128)}) %all-reduce.58.cloned.1.call-update) | async-done | bytes 262160 | tf_op jit(solution)/shard_map/psum | solution.py:31
  1350.3 84.5 %all-reduce.60.cloned.1.call-done = f32[1,1,256,256]{2,3,1,0:T(8,128)} async-done(((f32[1,1,256,256]{2,3,1,0:T(8,128)}), f32[1,1,256,256]{2,3,1,0:T(8,128)}) %all-reduce.60.cloned.1.call-update) | async-done | bytes 262160 | tf_op jit(solution)/shard_map/psum | solution.py:31
  1442.3 82.0 %all-reduce.62.cloned.1.call-done = f32[1,256,256]{1,2,0:T(8,128)} async-done(((f32[1,256,256]{1,2,0:T(8,128)}), f32[1,256,256]{1,2,0:T(8,128)}) %all-reduce.62.cloned.1.call-update) | async-done | bytes 262160 | tf_op jit(solution)/shard_map/psum | solution.py:31
  1534.6 85.1 %all-reduce.64.cloned.1.call-done = f32[2,1,256,256]{2,3,0,1:T(8,128)} async-done(((f32[2,1,256,256]{2,3,0,1:T(8,128)}), f32[2,1,256,256]{2,3,0,1:T(8,128)}) %all-reduce.64.cloned.1.call-update) | async-done | bytes 524304 | tf_op jit(solution)/shard_map/psum | solution.py:31
  1621.9 2.6 copy.114
  1629.1 3.4 scatter.106
  1632.5 81.6 %all-reduce.66.cloned.1.call-done = f32[2,1,256,256]{2,3,0,1:T(8,128)} async-done(((f32[2,1,256,256]{2,3,0,1:T(8,128)}), f32[2,1,256,256]{2,3,0,1:T(8,128)}) %all-reduce.66.cloned.1.call-update) | async-done | bytes 524304 | tf_op jit(solution)/shard_map/psum | solution.py:31
  1718.2 2.5 copy.115
  1725.3 85.2 %all-reduce.68.cloned.1.call-done = f32[2,1,256,256]{2,3,0,1:T(8,128)} async-done(((f32[2,1,256,256]{2,3,0,1:T(8,128)}), f32[2,1,256,256]{2,3,0,1:T(8,128)}) %all-reduce.68.cloned.1.call-update) | async-done | bytes 524304 | tf_op jit(solution)/shard_map/psum | solution.py:31
  1814.6 2.5 copy.116
  1821.7 85.2 %all-reduce.70.cloned.1.call-done = f32[2,1,256,256]{2,3,0,1:T(8,128)} async-done(((f32[2,1,256,256]{2,3,0,1:T(8,128)}), f32[2,1,256,256]{2,3,0,1:T(8,128)}) %all-reduce.70.cloned.1.call-update) | async-done | bytes 524304 | tf_op jit(solution)/shard_map/psum | solution.py:31
  1918.0 85.2 %all-reduce.72.cloned.1.call-done = f32[2,1,256,256]{2,3,0,1:T(8,128)} async-done(((f32[2,1,256,256]{2,3,0,1:T(8,128)}), f32[2,1,256,256]{2,3,0,1:T(8,128)}) %all-reduce.72.cloned.1.call-update) | async-done | bytes 524304 | tf_op jit(solution)/shard_map/psum | solution.py:31
  2014.4 85.3 %all-reduce.74.cloned.1.call-done = f32[2,1,256,256]{2,3,0,1:T(8,128)} async-done(((f32[2,1,256,256]{2,3,0,1:T(8,128)}), f32[2,1,256,256]{2,3,0,1:T(8,128)}) %all-reduce.74.cloned.1.call-update) | async-done | bytes 524304 | tf_op jit(solution)/shard_map/psum | solution.py:31
  2110.9 85.2 %all-reduce.76.cloned.1.call-done = f32[2,1,256,256]{2,3,0,1:T(8,128)} async-done(((f32[2,1,256,256]{2,3,0,1:T(8,128)}), f32[2,1,256,256]{2,3,0,1:T(8,128)}) %all-reduce.76.cloned.1.call-update) | async-done | bytes 524304 | tf_op jit(solution)/shard_map/psum | solution.py:31
  2208.7 83.8 %all-reduce.78.cloned.1.call-done = f32[2,1,256,256]{2,3,0,1:T(8,128)} async-done(((f32[2,1,256,256]{2,3,0,1:T(8,128)}), f32[2,1,256,256]{2,3,0,1:T(8,128)}) %all-reduce.78.cloned.1.call-update) | async-done | bytes 524304 | tf_op jit(solution)/shard_map/psum | solution.py:31
  (176 shorter events, 189.8 us)
Async XLA Ops:
  7.2 1521.5 %copy-start = (f32[1,2,8,64,256]{4,3,2,1,0:T(8,128)S(1)}, f32[1,2,8,64,256]{4,3,2,1,0:T(8,128)}, u32[]{:S(2)}) copy-start(f32[1,2,8,64,256]{4,3,2,1,0:T(8,128)} %param.63) | copy-start | bytes 3145732
  7.2 97.1 %all-reduce.30.cloned.1.call-start = ((), (), s32[]{:S(2)}) async-start(), calls=%async_computation | async-start | bytes 1048576 | tf_op jit(solution)/shard_map/psum | solution.py:31
  7.2 4.7 copy-start.3
  15.8 177.9 %all-reduce.32.cloned.1.call-start = ((), (), s32[]{:S(2)}) async-start(), calls=%async_computation.1 | async-start | bytes 1048576 | tf_op jit(solution)/shard_map/psum | solution.py:31
  109.6 176.9 %all-reduce.34.cloned.1.call-start = ((), (), s32[]{:S(2)}) async-start(), calls=%async_computation.2 | async-start | bytes 1048576 | tf_op jit(solution)/shard_map/psum | solution.py:31
  201.1 178.0 %all-reduce.36.cloned.1.call-start = ((), (), s32[]{:S(2)}) async-start(), calls=%async_computation.3 | async-start | bytes 1048576 | tf_op jit(solution)/shard_map/psum | solution.py:31
  293.9 178.0 %all-reduce.38.cloned.1.call-start = ((), (), s32[]{:S(2)}) async-start(), calls=%async_computation.4 | async-start | bytes 1048576 | tf_op jit(solution)/shard_map/psum | solution.py:31
  386.6 177.9 %all-reduce.40.cloned.1.call-start = ((), (), s32[]{:S(2)}) async-start(), calls=%async_computation.5 | async-start | bytes 1048576 | tf_op jit(solution)/shard_map/psum | solution.py:31
  479.3 177.9 %all-reduce.42.cloned.1.call-start = ((), (), s32[]{:S(2)}) async-start(), calls=%async_computation.6 | async-start | bytes 1048576 | tf_op jit(solution)/shard_map/psum | solution.py:31
  571.9 92.9 %copy-start.6 = (s32[1,4,2]{1,2,0:T(2,128)S(1)}, s32[1,4,2]{1,2,0:T(2,128)}, u32[]{:S(2)}) copy-start(s32[1,4,2]{1,2,0:T(2,128)} %param.64) | copy-start | bytes 100
  571.9 93.0 %copy-start.5 = (f32[4,64,32]{1,2,0:T(8,128)S(1)}, f32[4,64,32]{1,2,0:T(8,128)}, u32[]{:S(2)}) copy-start(f32[4,64,32]{1,2,0:T(8,128)} %param.69) | copy-start | bytes 98308
  571.9 177.9 %all-reduce.44.cloned.1.call-start = ((), (), s32[]{:S(2)}) async-start(), calls=%async_computation.7 | async-start | bytes 1048576 | tf_op jit(solution)/shard_map/psum | solution.py:31
  664.6 150.2 %all-reduce.46.cloned.1.call-start = ((), (), s32[]{:S(2)}) async-start(), calls=%async_computation.8 | async-start | bytes 524288 | tf_op jit(solution)/shard_map/psum | solution.py:73
  749.8 3.4 copy-start.1
  755.0 147.5 %all-reduce.48.cloned.1.call-start = ((), (), s32[]{:S(2)}) async-start(), calls=%async_computation.9 | async-start | bytes 524288 | tf_op jit(solution)/shard_map/psum | solution.py:31
  816.8 173.4 %all-reduce.50.cloned.1.call-start = ((), (), s32[]{:S(2)}) async-start(), calls=%async_computation.10 | async-start | bytes 524288 | tf_op jit(solution)/shard_map/psum | solution.py:31
  905.8 173.9 %all-reduce.52.cloned.1.call-start = ((), (), s32[]{:S(2)}) async-start(), calls=%async_computation.11 | async-start | bytes 524288 | tf_op jit(solution)/shard_map/psum | solution.py:31
  995.1 174.0 %all-reduce.54.cloned.1.call-start = ((), (), s32[]{:S(2)}) async-start(), calls=%async_computation.12 | async-start | bytes 524288 | tf_op jit(solution)/shard_map/psum | solution.py:31
  1082.6 264.3 %copy-start.4 = (f32[4,64,256]{2,1,0:T(8,128)S(1)}, f32[4,64,256]{2,1,0:T(8,128)}, u32[]{:S(2)}) copy-start(f32[4,64,256]{2,1,0:T(8,128)} %param.65) | copy-start | bytes 786436
  1084.7 172.8 %all-reduce.56.cloned.1.call-start = ((), (), s32[]{:S(2)}) async-start(), calls=%async_computation.13 | async-start | bytes 524288 | tf_op jit(solution)/shard_map/psum | solution.py:31
  1172.9 172.3 %all-reduce.58.cloned.1.call-start = ((), (), s32[]{:S(2)}) async-start(), calls=%async_computation.14 | async-start | bytes 524288 | tf_op jit(solution)/shard_map/psum | solution.py:31
  1260.7 174.1 %all-reduce.60.cloned.1.call-start = ((), (), s32[]{:S(2)}) async-start(), calls=%async_computation.15 | async-start | bytes 524288 | tf_op jit(solution)/shard_map/psum | solution.py:31
  1350.2 174.0 %all-reduce.62.cloned.1.call-start = ((), (), s32[]{:S(2)}) async-start(), calls=%async_computation.16 | async-start | bytes 524288 | tf_op jit(solution)/shard_map/psum | solution.py:31
  1439.8 180.0 %all-reduce.64.cloned.1.call-start = ((), (), s32[]{:S(2)}) async-start(), calls=%async_computation.17 | async-start | bytes 1048576 | tf_op jit(solution)/shard_map/psum | solution.py:31
  1529.9 1.1 copy-start.2
  1534.6 179.5 %all-reduce.66.cloned.1.call-start = ((), (), s32[]{:S(2)}) async-start(), calls=%async_computation.18 | async-start | bytes 1048576 | tf_op jit(solution)/shard_map/psum | solution.py:31
  1628.9 181.6 %all-reduce.68.cloned.1.call-start = ((), (), s32[]{:S(2)}) async-start(), calls=%async_computation.19 | async-start | bytes 1048576 | tf_op jit(solution)/shard_map/psum | solution.py:31
  1725.2 181.6 %all-reduce.70.cloned.1.call-start = ((), (), s32[]{:S(2)}) async-start(), calls=%async_computation.20 | async-start | bytes 1048576 | tf_op jit(solution)/shard_map/psum | solution.py:31
  1821.6 181.6 %all-reduce.72.cloned.1.call-start = ((), (), s32[]{:S(2)}) async-start(), calls=%async_computation.21 | async-start | bytes 1048576 | tf_op jit(solution)/shard_map/psum | solution.py:31
  1918.0 181.7 %all-reduce.74.cloned.1.call-start = ((), (), s32[]{:S(2)}) async-start(), calls=%async_computation.22 | async-start | bytes 1048576 | tf_op jit(solution)/shard_map/psum | solution.py:31
  2014.3 181.7 %all-reduce.76.cloned.1.call-start = ((), (), s32[]{:S(2)}) async-start(), calls=%async_computation.23 | async-start | bytes 1048576 | tf_op jit(solution)/shard_map/psum | solution.py:31
  2110.8 181.7 %all-reduce.78.cloned.1.call-start = ((), (), s32[]{:S(2)}) async-start(), calls=%async_computation.24 | async-start | bytes 1048576 | tf_op jit(solution)/shard_map/psum | solution.py:31
Sparse Core Ops, SparseCore 0:
  15.9 88.3 all-reduce.29
  109.7 84.0 all-reduce.31
  201.3 85.1 all-reduce.33
  294.0 85.1 all-reduce.35
  386.7 85.1 all-reduce.37
  479.4 85.0 all-reduce.39
  572.0 85.1 all-reduce.41
  664.7 85.0 all-reduce.43
  755.1 59.5 all-reduce.45
  818.3 84.1 all-reduce.47
  905.9 84.2 all-reduce.49
  995.3 84.3 all-reduce.51
  1084.8 84.3 all-reduce.53
  1173.1 84.3 all-reduce.55
  1260.8 84.3 all-reduce.57
  1350.4 84.3 all-reduce.59
  1439.9 84.3 all-reduce.61
  1534.7 85.0 all-reduce.63
  1629.0 85.0 all-reduce.65
  1725.3 85.0 all-reduce.67
  1821.7 85.0 all-reduce.69
  1918.1 85.0 all-reduce.71
  2014.5 85.1 all-reduce.73
  2110.9 85.0 all-reduce.75
  2207.4 85.0 all-reduce.77
where the time goes:
time: 2310 us; the launch traced here: 2300 us
  waiting for transfers between devices  2070 us (90%)
  local copies, waits for them, and re-layouts  108 us (5%)
  matrix products  93 us (4%)
    psum x24, waiting for transfers between devices, sweep_blocks(): block_value = lax.psum(inverse_part, ('prow', 'pcol'))  2020 us
    dot_general x24, matrix products, sweep_blocks(): jnp.einsum('gab,gar->gbr', inverses[:, sweep_step_index], local_side, pre...  53.3 us
    scatter x24, local copies, waits for them, and re-layouts, sweep_blocks(): solved = solved.at[:, sweep_step_index].set(block_value)  47.2 us
  transfers between devices with their start and end apart: 25, of which 25 were waited for; matrix products, arithmetic and copies ran while one was open for 1% of the time, Pallas kernels for 0%

commit v1 on v0

--- a/solution.py
+++ b/solution.py
@@ -28,7 +28,7 @@
         inverse_part = jnp.einsum(
             "gab,gar->gbr", inverses[:, sweep_step_index], local_side, precision=TOP_PRECISION
         )
-        block_value = lax.psum(inverse_part, ("prow", "pcol"))
+        block_value = lax.psum(lax.psum(inverse_part, "pcol"), "prow")
         solved = solved.at[:, sweep_step_index].set(block_value)
     return solved
 

time: 2310 us -> 2400 us (1.039)
  waiting for transfers between devices: 2070 us -> 2160 us
    psum x24 -> x48, waiting for transfers between devices: 2020 us -> 2120 us  [sweep_blocks(): block_value = lax.psum(lax.psum(inverse_part, 'pcol'), 'prow')]
  transfers between devices with their start and end apart: 25 -> 49, of which waited for: 25 -> 49; matrix products, arithmetic and copies ran while one was open for 1% -> 1% of each run, Pallas kernels for 0% -> 0%
where the time goes in v1:
time: 2400 us
  waiting for transfers between devices  2160 us (90%)
  local copies, waits for them, and re-layouts  108 us (4%)
  matrix products  93 us (4%)
    psum x48, waiting for transfers between devices, sweep_blocks(): block_value = lax.psum(lax.psum(inverse_part, 'pcol'), 'prow')  2120 us
    dot_general x24, matrix products, sweep_blocks(): jnp.einsum('gab,gar->gbr', inverses[:, sweep_step_index], local_side, pre...  53.4 us
  transfers between devices with their start and end apart: 49, of which 49 were waited for; matrix products, arithmetic and copies ran while one was open for 1% of the time, Pallas kernels for 0%

profile of v1, /device:TPU:0, one launch (start us, length us, event | category | flops | bytes accessed | tf_op | source)
XLA Modules:
  0.0 2400.3 jit_solution(1151311151271409800)
XLA Ops:
  15.9 45.6 %all-reduce.54.cloned.1.call-done = f32[2,256,256]{2,1,0:T(8,128)} async-done(((f32[2,256,256]{2,1,0:T(8,128)}), f32[2,256,256]{2,1,0:T(8,128)}) %all-reduce.54.cloned.1.call-update) | async-done | bytes 524304 | tf_op jit(solution)/shard_map/psum | solution.py:31
  61.6 46.2 %all-reduce.56.cloned.1.call-done = f32[2,1,256,256]{3,2,0,1:T(8,128)} async-done(((f32[2,1,256,256]{3,2,0,1:T(8,128)}), f32[2,1,256,256]{3,2,0,1:T(8,128)}) %all-reduce.56.cloned.1.call-update) | async-done | bytes 524304 | tf_op jit(solution)/shard_map/psum | solution.py:31
  253.4 46.1 %all-reduce.64.cloned.1.call-done = f32[2,1,256,256]{3,2,0,1:T(8,128)} async-done(((f32[2,1,256,256]{3,2,0,1:T(8,128)}), f32[2,1,256,256]{3,2,0,1:T(8,128)}) %all-reduce.64.cloned.1.call-update) | async-done | bytes 524304 | tf_op jit(solution)/shard_map/psum | solution.py:31
  306.9 43.8 %all-reduce.66.cloned.1.call-done = f32[2,256,256]{2,1,0:T(8,128)} async-done(((f32[2,256,256]{2,1,0:T(8,128)}), f32[2,256,256]{2,1,0:T(8,128)}) %all-reduce.66.cloned.1.call-update) | async-done | bytes 524304 | tf_op jit(solution)/shard_map/psum | solution.py:31
  350.8 46.2 %all-reduce.68.cloned.1.call-done = f32[2,1,256,256]{3,2,0,1:T(8,128)} async-done(((f32[2,1,256,256]{3,2,0,1:T(8,128)}), f32[2,1,256,256]{3,2,0,1:T(8,128)}) %all-reduce.68.cloned.1.call-update) | async-done | bytes 524304 | tf_op jit(solution)/shard_map/psum | solution.py:31
  404.4 43.8 %all-reduce.70.cloned.1.call-done = f32[2,256,256]{2,1,0:T(8,128)} async-done(((f32[2,256,256]{2,1,0:T(8,128)}), f32[2,256,256]{2,1,0:T(8,128)}) %all-reduce.70.cloned.1.call-update) | async-done | bytes 524304 | tf_op jit(solution)/shard_map/psum | solution.py:31
  448.3 46.1 %all-reduce.72.cloned.1.call-done = f32[2,1,256,256]{3,2,0,1:T(8,128)} async-done(((f32[2,1,256,256]{3,2,0,1:T(8,128)}), f32[2,1,256,256]{3,2,0,1:T(8,128)}) %all-reduce.72.cloned.1.call-update) | async-done | bytes 524304 | tf_op jit(solution)/shard_map/psum | solution.py:31
  501.8 43.8 %all-reduce.74.cloned.1.call-done = f32[2,256,256]{2,1,0:T(8,128)} async-done(((f32[2,256,256]{2,1,0:T(8,128)}), f32[2,256,256]{2,1,0:T(8,128)}) %all-reduce.74.cloned.1.call-update) | async-done | bytes 524304 | tf_op jit(solution)/shard_map/psum | solution.py:31
  545.7 46.1 %all-reduce.76.cloned.1.call-done = f32[2,1,256,256]{3,2,0,1:T(8,128)} async-done(((f32[2,1,256,256]{3,2,0,1:T(8,128)}), f32[2,1,256,256]{3,2,0,1:T(8,128)}) %all-reduce.76.cloned.1.call-update) | async-done | bytes 524304 | tf_op jit(solution)/shard_map/psum | solution.py:31
  599.2 43.8 %all-reduce.78.cloned.1.call-done = f32[2,256,256]{2,1,0:T(8,128)} async-done(((f32[2,256,256]{2,1,0:T(8,128)}), f32[2,256,256]{2,1,0:T(8,128)}) %all-reduce.78.cloned.1.call-update) | async-done | bytes 524304 | tf_op jit(solution)/shard_map/psum | solution.py:31
  643.3 45.9 %all-reduce.80.cloned.1.call-done = f32[2,1,256,256]{3,2,0,1:T(8,128)} async-done(((f32[2,1,256,256]{3,2,0,1:T(8,128)}), f32[2,1,256,256]{3,2,0,1:T(8,128)}) %all-reduce.80.cloned.1.call-update) | async-done | bytes 524304 | tf_op jit(solution)/shard_map/psum | solution.py:31
  696.5 43.8 %all-reduce.82.cloned.1.call-done = f32[2,256,256]{2,1,0:T(8,128)} async-done(((f32[2,256,256]{2,1,0:T(8,128)}), f32[2,256,256]{2,1,0:T(8,128)}) %all-reduce.82.cloned.1.call-update) | async-done | bytes 524304 | tf_op jit(solution)/shard_map/psum | solution.py:31
  808.5 44.2 %all-reduce.86.cloned.1.call-done = f32[1,4,64,256]{3,2,1,0:T(8,128)} async-done(((f32[1,4,64,256]{3,2,1,0:T(8,128)}), f32[1,4,64,256]{3,2,1,0:T(8,128)}) %all-reduce.86.cloned.1.call-update) | async-done | bytes 262160 | tf_op jit(solution)/shard_map/psum | solution.py:73
  896.5 44.9 %all-reduce.90.cloned.1.call-done = f32[1,1,256,256]{3,2,1,0:T(8,128)} async-done(((f32[1,1,256,256]{3,2,1,0:T(8,128)}), f32[1,1,256,256]{3,2,1,0:T(8,128)}) %all-reduce.90.cloned.1.call-update) | async-done | bytes 262160 | tf_op jit(solution)/shard_map/psum | solution.py:31
  1079.2 44.9 %all-reduce.98.cloned.1.call-done = f32[1,1,256,256]{3,2,1,0:T(8,128)} async-done(((f32[1,1,256,256]{3,2,1,0:T(8,128)}), f32[1,1,256,256]{3,2,1,0:T(8,128)}) %all-reduce.98.cloned.1.call-update) | async-done | bytes 262160 | tf_op jit(solution)/shard_map/psum | solution.py:31
  1171.5 44.9 %all-reduce.102.cloned.1.call-done = f32[1,1,256,256]{3,2,1,0:T(8,128)} async-done(((f32[1,1,256,256]{3,2,1,0:T(8,128)}), f32[1,1,256,256]{3,2,1,0:T(8,128)}) %all-reduce.102.cloned.1.call-update) | async-done | bytes 262160 | tf_op jit(solution)/shard_map/psum | solution.py:31
  1262.6 44.7 %all-reduce.106.cloned.1.call-done = f32[1,1,256,256]{2,3,1,0:T(8,128)} async-done(((f32[1,1,256,256]{2,3,1,0:T(8,128)}), f32[1,1,256,256]{2,3,1,0:T(8,128)}) %all-reduce.106.cloned.1.call-update) | async-done | bytes 262160 | tf_op jit(solution)/shard_map/psum | solution.py:31
  1445.3 44.9 %all-reduce.114.cloned.1.call-done = f32[1,1,256,256]{2,3,1,0:T(8,128)} async-done(((f32[1,1,256,256]{2,3,1,0:T(8,128)}), f32[1,1,256,256]{2,3,1,0:T(8,128)}) %all-reduce.114.cloned.1.call-update) | async-done | bytes 262160 | tf_op jit(solution)/shard_map/psum | solution.py:31
  1636.6 46.0 %all-reduce.122.cloned.1.call-done = f32[2,1,256,256]{2,3,0,1:T(8,128)} async-done(((f32[2,1,256,256]{2,3,0,1:T(8,128)}), f32[2,1,256,256]{2,3,0,1:T(8,128)}) %all-reduce.122.cloned.1.call-update) | async-done | bytes 524304 | tf_op jit(solution)/shard_map/psum | solution.py:31
  1691.7 43.8 %all-reduce.124.cloned.1.call-done = f32[2,256,256]{1,2,0:T(8,128)} async-done(((f32[2,256,256]{1,2,0:T(8,128)}), f32[2,256,256]{1,2,0:T(8,128)}) %all-reduce.124.cloned.1.call-update) | async-done | bytes 524304 | tf_op jit(solution)/shard_map/psum | solution.py:31
  1792.9 43.8 %all-reduce.128.cloned.1.call-done = f32[2,256,256]{1,2,0:T(8,128)} async-done(((f32[2,256,256]{1,2,0:T(8,128)}), f32[2,256,256]{1,2,0:T(8,128)}) %all-reduce.128.cloned.1.call-update) | async-done | bytes 524304 | tf_op jit(solution)/shard_map/psum | solution.py:31
  1836.8 46.1 %all-reduce.130.cloned.1.call-done = f32[2,1,256,256]{2,3,0,1:T(8,128)} async-done(((f32[2,1,256,256]{2,3,0,1:T(8,128)}), f32[2,1,256,256]{2,3,0,1:T(8,128)}) %all-reduce.130.cloned.1.call-update) | async-done | bytes 524304 | tf_op jit(solution)/shard_map/psum | solution.py:31
  1894.1 43.8 %all-reduce.132.cloned.1.call-done = f32[2,256,256]{1,2,0:T(8,128)} async-done(((f32[2,256,256]{1,2,0:T(8,128)}), f32[2,256,256]{1,2,0:T(8,128)}) %all-reduce.132.cloned.1.call-update) | async-done | bytes 524304 | tf_op jit(solution)/shard_map/psum | solution.py:31
  1938.0 46.2 %all-reduce.134.cloned.1.call-done = f32[2,1,256,256]{2,3,0,1:T(8,128)} async-done(((f32[2,1,256,256]{2,3,0,1:T(8,128)}), f32[2,1,256,256]{2,3,0,1:T(8,128)}) %all-reduce.134.cloned.1.call-update) | async-done | bytes 524304 | tf_op jit(solution)/shard_map/psum | solution.py:31
  1995.4 43.8 %all-reduce.136.cloned.1.call-done = f32[2,256,256]{1,2,0:T(8,128)} async-done(((f32[2,256,256]{1,2,0:T(8,128)}), f32[2,256,256]{1,2,0:T(8,128)}) %all-reduce.136.cloned.1.call-update) | async-done | bytes 524304 | tf_op jit(solution)/shard_map/psum | solution.py:31
  2039.3 46.1 %all-reduce.138.cloned.1.call-done = f32[2,1,256,256]{2,3,0,1:T(8,128)} async-done(((f32[2,1,256,256]{2,3,0,1:T(8,128)}), f32[2,1,256,256]{2,3,0,1:T(8,128)}) %all-reduce.138.cloned.1.call-update) | async-done | bytes 524304 | tf_op jit(solution)/shard_map/psum | solution.py:31
  2096.6 43.8 %all-reduce.140.cloned.1.call-done = f32[2,256,256]{1,2,0:T(8,128)} async-done(((f32[2,256,256]{1,2,0:T(8,128)}), f32[2,256,256]{1,2,0:T(8,128)}) %all-reduce.140.cloned.1.call-update) | async-done | bytes 524304 | tf_op jit(solution)/shard_map/psum | solution.py:31
  2140.5 46.1 %all-reduce.142.cloned.1.call-done = f32[2,1,256,256]{2,3,0,1:T(8,128)} async-done(((f32[2,1,256,256]{2,3,0,1:T(8,128)}), f32[2,1,256,256]{2,3,0,1:T(8,128)}) %all-reduce.142.cloned.1.call-update) | async-done | bytes 524304 | tf_op jit(solution)/shard_map/psum | solution.py:31
  2197.8 43.8 %all-reduce.144.cloned.1.call-done = f32[2,256,256]{1,2,0:T(8,128)} async-done(((f32[2,256,256]{1,2,0:T(8,128)}), f32[2,256,256]{1,2,0:T(8,128)}) %all-reduce.144.cloned.1.call-update) | async-done | bytes 524304 | tf_op jit(solution)/shard_map/psum | solution.py:31
  2241.6 46.1 %all-reduce.146.cloned.1.call-done = f32[2,1,256,256]{2,3,0,1:T(8,128)} async-done(((f32[2,1,256,256]{2,3,0,1:T(8,128)}), f32[2,1,256,256]{2,3,0,1:T(8,128)}) %all-reduce.146.cloned.1.call-update) | async-done | bytes 524304 | tf_op jit(solution)/shard_map/psum | solution.py:31
  2299.0 43.8 %all-reduce.148.cloned.1.call-done = f32[2,256,256]{1,2,0:T(8,128)} async-done(((f32[2,256,256]{1,2,0:T(8,128)}), f32[2,256,256]{1,2,0:T(8,128)}) %all-reduce.148.cloned.1.call-update) | async-done | bytes 524304 | tf_op jit(solution)/shard_map/psum | solution.py:31
  2344.2 44.7 %all-reduce.150.cloned.1.call-done = f32[2,1,256,256]{2,3,0,1:T(8,128)} async-done(((f32[2,1,256,256]{2,3,0,1:T(8,128)}), f32[2,1,256,256]{2,3,0,1:T(8,128)}) %all-reduce.150.cloned.1.call-update) | async-done | bytes 524304 | tf_op jit(solution)/shard_map/psum | solution.py:31
  (248 shorter events, 947.4 us)
Async XLA Ops:
  15.8 92.0 %all-reduce.56.cloned.1.call-start = ((), (), s32[]{:S(2)}) async-start(), calls=%async_computation.1 | async-start | bytes 1048576 | tf_op jit(solution)/shard_map/psum | solution.py:31
  61.6 94.4 %all-reduce.58.cloned.1.call-start = ((), (), s32[]{:S(2)}) async-start(), calls=%async_computation.2 | async-start | bytes 1048576 | tf_op jit(solution)/shard_map/psum | solution.py:31
  156.0 97.4 %all-reduce.62.cloned.1.call-start = ((), (), s32[]{:S(2)}) async-start(), calls=%async_computation.4 | async-start | bytes 1048576 | tf_op jit(solution)/shard_map/psum | solution.py:31
  253.3 97.4 %all-reduce.66.cloned.1.call-start = ((), (), s32[]{:S(2)}) async-start(), calls=%async_computation.6 | async-start | bytes 1048576 | tf_op jit(solution)/shard_map/psum | solution.py:31
  306.9 90.2 %all-reduce.68.cloned.1.call-start = ((), (), s32[]{:S(2)}) async-start(), calls=%async_computation.7 | async-start | bytes 1048576 | tf_op jit(solution)/shard_map/psum | solution.py:31
  350.7 97.5 %all-reduce.70.cloned.1.call-start = ((), (), s32[]{:S(2)}) async-start(), calls=%async_computation.8 | async-start | bytes 1048576 | tf_op jit(solution)/shard_map/psum | solution.py:31
  448.3 97.3 %all-reduce.74.cloned.1.call-start = ((), (), s32[]{:S(2)}) async-start(), calls=%async_computation.10 | async-start | bytes 1048576 | tf_op jit(solution)/shard_map/psum | solution.py:31
  501.8 90.0 %all-reduce.76.cloned.1.call-start = ((), (), s32[]{:S(2)}) async-start(), calls=%async_computation.11 | async-start | bytes 1048576 | tf_op jit(solution)/shard_map/psum | solution.py:31
  545.6 97.4 %all-reduce.78.cloned.1.call-start = ((), (), s32[]{:S(2)}) async-start(), calls=%async_computation.12 | async-start | bytes 1048576 | tf_op jit(solution)/shard_map/psum | solution.py:31
  643.0 97.3 %all-reduce.82.cloned.1.call-start = ((), (), s32[]{:S(2)}) async-start(), calls=%async_computation.14 | async-start | bytes 1048576 | tf_op jit(solution)/shard_map/psum | solution.py:31
  696.5 90.0 %all-reduce.84.cloned.1.call-start = ((), (), s32[]{:S(2)}) async-start(), calls=%async_computation.15 | async-start | bytes 1048576 | tf_op jit(solution)/shard_map/psum | solution.py:31
  740.4 112.4 %all-reduce.86.cloned.1.call-start = ((), (), s32[]{:S(2)}) async-start(), calls=%async_computation.16 | async-start | bytes 524288 | tf_op jit(solution)/shard_map/psum | solution.py:73
  791.7 104.7 %all-reduce.88.cloned.1.call-start = ((), (), s32[]{:S(2)}) async-start(), calls=%async_computation.17 | async-start | bytes 524288 | tf_op jit(solution)/shard_map/psum | solution.py:31
  896.5 90.4 %all-reduce.92.cloned.1.call-start = ((), (), s32[]{:S(2)}) async-start(), calls=%async_computation.19 | async-start | bytes 524288 | tf_op jit(solution)/shard_map/psum | solution.py:31
  986.9 92.2 %all-reduce.96.cloned.1.call-start = ((), (), s32[]{:S(2)}) async-start(), calls=%async_computation.21 | async-start | bytes 524288 | tf_op jit(solution)/shard_map/psum | solution.py:31
  1079.2 92.3 %all-reduce.100.cloned.1.call-start = ((), (), s32[]{:S(2)}) async-start(), calls=%async_computation.23 | async-start | bytes 524288 | tf_op jit(solution)/shard_map/psum | solution.py:31
  1171.5 91.0 %all-reduce.104.cloned.1.call-start = ((), (), s32[]{:S(2)}) async-start(), calls=%async_computation.25 | async-start | bytes 524288 | tf_op jit(solution)/shard_map/psum | solution.py:31
  1262.5 90.4 %all-reduce.108.cloned.1.call-start = ((), (), s32[]{:S(2)}) async-start(), calls=%async_computation.27 | async-start | bytes 524288 | tf_op jit(solution)/shard_map/psum | solution.py:31
  1353.0 92.3 %all-reduce.112.cloned.1.call-start = ((), (), s32[]{:S(2)}) async-start(), calls=%async_computation.29 | async-start | bytes 524288 | tf_op jit(solution)/shard_map/psum | solution.py:31
  1445.3 92.3 %all-reduce.116.cloned.1.call-start = ((), (), s32[]{:S(2)}) async-start(), calls=%async_computation.31 | async-start | bytes 524288 | tf_op jit(solution)/shard_map/psum | solution.py:31
  1537.6 98.7 %all-reduce.120.cloned.1.call-start = ((), (), s32[]{:S(2)}) async-start(), calls=%async_computation.33 | async-start | bytes 1048576 | tf_op jit(solution)/shard_map/psum | solution.py:31
  1636.3 99.2 %all-reduce.124.cloned.1.call-start = ((), (), s32[]{:S(2)}) async-start(), calls=%async_computation.35 | async-start | bytes 1048576 | tf_op jit(solution)/shard_map/psum | solution.py:31
  1691.7 90.0 %all-reduce.126.cloned.1.call-start = ((), (), s32[]{:S(2)}) async-start(), calls=%async_computation.36 | async-start | bytes 1048576 | tf_op jit(solution)/shard_map/psum | solution.py:31
  1735.6 101.1 %all-reduce.128.cloned.1.call-start = ((), (), s32[]{:S(2)}) async-start(), calls=%async_computation.37 | async-start | bytes 1048576 | tf_op jit(solution)/shard_map/psum | solution.py:31
  1836.7 101.2 %all-reduce.132.cloned.1.call-start = ((), (), s32[]{:S(2)}) async-start(), calls=%async_computation.39 | async-start | bytes 1048576 | tf_op jit(solution)/shard_map/psum | solution.py:31
  1894.1 90.2 %all-reduce.134.cloned.1.call-start = ((), (), s32[]{:S(2)}) async-start(), calls=%async_computation.40 | async-start | bytes 1048576 | tf_op jit(solution)/shard_map/psum | solution.py:31
  1937.9 101.3 %all-reduce.136.cloned.1.call-start = ((), (), s32[]{:S(2)}) async-start(), calls=%async_computation.41 | async-start | bytes 1048576 | tf_op jit(solution)/shard_map/psum | solution.py:31
  2039.2 101.1 %all-reduce.140.cloned.1.call-start = ((), (), s32[]{:S(2)}) async-start(), calls=%async_computation.43 | async-start | bytes 1048576 | tf_op jit(solution)/shard_map/psum | solution.py:31
  2140.4 101.1 %all-reduce.144.cloned.1.call-start = ((), (), s32[]{:S(2)}) async-start(), calls=%async_computation.45 | async-start | bytes 1048576 | tf_op jit(solution)/shard_map/psum | solution.py:31
  2197.7 90.0 %all-reduce.146.cloned.1.call-start = ((), (), s32[]{:S(2)}) async-start(), calls=%async_computation.46 | async-start | bytes 1048576 | tf_op jit(solution)/shard_map/psum | solution.py:31
  2241.6 101.2 %all-reduce.148.cloned.1.call-start = ((), (), s32[]{:S(2)}) async-start(), calls=%async_computation.47 | async-start | bytes 1048576 | tf_op jit(solution)/shard_map/psum | solution.py:31
  2298.9 90.0 %all-reduce.150.cloned.1.call-start = ((), (), s32[]{:S(2)}) async-start(), calls=%async_computation.48 | async-start | bytes 1048576 | tf_op jit(solution)/shard_map/psum | solution.py:31
  (24 other events, 3527.0 us)
Sparse Core Ops, SparseCore 0:
  16.0 45.5 all-reduce.53
  63.9 43.9 all-reduce.55
  158.1 43.9 all-reduce.59
  209.6 43.6 all-reduce.61
  255.5 43.9 all-reduce.63
  307.0 43.6 all-reduce.65
  353.1 43.9 all-reduce.67
  404.5 43.6 all-reduce.69
  450.4 43.9 all-reduce.71
  501.9 43.6 all-reduce.73
  547.8 43.9 all-reduce.75
  599.3 43.6 all-reduce.77
  645.2 43.9 all-reduce.79
  696.6 43.6 all-reduce.81
  742.5 43.9 all-reduce.83
  791.8 60.8 all-reduce.85
  1592.8 43.4 all-reduce.119
  1638.6 43.9 all-reduce.121
  1691.8 43.6 all-reduce.123
  1737.8 43.9 all-reduce.125
  1793.0 43.6 all-reduce.127
  1838.9 43.9 all-reduce.129
  1894.2 43.6 all-reduce.131
  1940.2 43.9 all-reduce.133
  1995.5 43.6 all-reduce.135
  2041.4 43.9 all-reduce.137
  2096.7 43.6 all-reduce.139
  2142.6 43.9 all-reduce.141
  2197.8 43.6 all-reduce.143
  2243.8 43.9 all-reduce.145
  2299.0 43.6 all-reduce.147
  2344.9 43.9 all-reduce.149
  (17 shorter events, 718.6 us)
